TPU v7x, 32 devices: a whole 2x2x4 slice. The times are simulated.
32 devices in a mesh: groups: 2 (over y), feat: 4 (over z), tok: 2 (over x), rep: 2 (over core).
Axes of the slice: x: 2, y: 2, z: 4, core: 2. Of those that a mesh axis runs over, the one named last changes fastest.
Arguments:
- tokens: bfloat16 [448, 8192], P(('groups', 'tok', 'rep'), 'feat'), parts along dimension 0, may hold values from -6 to 6
- gate_weight: bfloat16 [8192, 14336], P('feat', ('tok', 'rep')), may hold values from -0.09375 to 0.09375
- up_weight: bfloat16 [8192, 14336], P('feat', ('tok', 'rep')), may hold values from -0.09375 to 0.09375
- down_weight: bfloat16 [14336, 8192], P(('tok', 'rep'), 'feat'), may hold values from -0.0625 to 0.0625
- gate_mask: int32 [64, 112], P('feat', ('tok', 'rep')), may hold values 0 or 1
- up_mask: int32 [64, 112], P('feat', ('tok', 'rep')), may hold values 0 or 1
- down_mask: int32 [112, 64], P(('tok', 'rep'), 'feat'), may hold values 0 or 1
Outputs:
- mixed: bfloat16 [448, 8192], P(('groups', 'tok', 'rep'), 'feat'), parts along dimension 0
There are 2 independent parts, one for each index of `groups`. A program takes and returns all parts, laid end to end along the dimension named above; an argument that names none is the same for every part. Nothing has to cross between parts.
Inputs may be any that keep to these rules, and one draw needn't show every extreme that they name: `gate_mask`: entries are 0 or 1; 1 keeps the block. `up_mask`: entries are 0 or 1; 1 keeps the block. `down_mask`: entries are 0 or 1; 1 keeps the block.
All inputs are finite; a program needn't handle non-finite values.
Results may differ from a plain program's by a relative error of at most 0.02.
Values may be sent and summed in bfloat16 or wider, within the bound.
A program may use at most 192 MiB of HBM per device.

v0:
```python
import jax
import jax.numpy as jnp
from jax import lax
from jax.sharding import PartitionSpec as P

BLOCK = 128


def expand(mask_grid):
    return jnp.repeat(jnp.repeat(mask_grid.astype(jnp.bfloat16), BLOCK, 0), BLOCK, 1)


def shards(tokens, gate_weight, up_weight, down_weight, gate_mask, up_mask, down_mask):
    gate_kept = gate_weight * expand(gate_mask)
    up_kept = up_weight * expand(up_mask)
    down_kept = down_weight * expand(down_mask)
    stacked = jnp.concatenate([gate_kept, up_kept], axis=1)
    hidden_cols = gate_kept.shape[1]
    partial_value = jnp.dot(
        lax.all_gather(tokens, ("tok", "rep"), axis=0, tiled=True),
        stacked,
        preferred_element_type=jnp.float32,
    )
    totals = lax.psum(partial_value.astype(jnp.bfloat16), "feat").astype(jnp.float32)
    hidden = (jax.nn.silu(totals[:, :hidden_cols]) * totals[:, hidden_cols:]).astype(jnp.bfloat16)
    return lax.psum_scatter(
        jnp.dot(hidden, down_kept, preferred_element_type=jnp.float32).astype(jnp.bfloat16),
        ("tok", "rep"),
        scatter_dimension=0,
        tiled=True,
    )


def solution(mesh):
    return jax.shard_map(
        shards,
        mesh=mesh,
        in_specs=(
            P(("groups", "tok", "rep"), "feat"),
            P("feat", ("tok", "rep")),
            P("feat", ("tok", "rep")),
            P(("tok", "rep"), "feat"),
            P("feat", ("tok", "rep")),
            P("feat", ("tok", "rep")),
            P(("tok", "rep"), "feat"),
        ),
        out_specs=P(("groups", "tok", "rep"), "feat"),
        check_vma=False,
    )
```

profile of v0, /device:TPU:0, one launch (start us, length us, event | category | flops | bytes accessed | tf_op | source)
XLA Modules:
  0.0 276.7 jit_solution(15015682592112196510)
XLA Ops:
  6.5 0.0 all-reduce.2.cloned.1.call-start
  6.5 20.4 %copy.10 = bf16[2048,3584]{0,1:T(8,128)(2,1)} copy(bf16[2048,3584]{1,0:T(8,128)(2,1)} %param.8) | data formatting | bytes 29360128 | tf_op args[1]
  26.9 0.0 copy-start.1
  26.9 0.0 copy-start.2
  26.9 0.0 copy-start
  26.9 20.4 %copy.12 = bf16[2048,3584]{0,1:T(8,128)(2,1)} copy(bf16[2048,3584]{1,0:T(8,128)(2,1)} %param.9) | data formatting | bytes 29360128 | tf_op args[2]
  47.3 0.0 copy-done.1
  47.3 0.1 copy.11
  47.4 0.1 broadcast_bitcast_fusion
  47.6 0.0 copy-done.2
  47.6 0.1 copy.9
  47.7 0.1 broadcast_bitcast_fusion.1
  47.9 0.0 copy-done
  47.9 10.8 %all_gather.3 = bf16[224,2048]{1,0:T(8,128)(2,1)S(1)} all-gather(bf16[56,2048]{1,0:T(8,128)(2,1)S(1)} %copy-done), channel_id=1, replica_groups=mesh['groups'=2,'feat'=4,'tok'=2,'rep'=2] {'tok','rep'}, dimensions={0}, use_global_device_ids=true | all-gather | bytes 1146880 | tf_op jit(solution)/shard_map/all_gather | solution.py:20
  58.7 21.4 %bitcast_multiply_fusion.2 = (bf16[2048,3584]{0,1:T(8,128)(2,1)}, bf16[2048,3584]{0,1:T(8,128)(2,1)}) fusion(bf16[2048,3584]{0,1:T(8,128)(2,1)} %copy.12, bf16[2048,28]{0,1:T(8,128)(2,1)S(1)} %bitcast.28, bf16[2048,3584]{0,1:T(8,128)(2,1)} %copy.10, bf16[2048,28]{0,1:T(8,128)(2,1)S(1)} %bitcast.29), kind=kLoop, calls=%fused_computation.7 | loop fusion | flops 14680064 | bytes 58949632 | tf_op jit(solution)/shard_map/mul | solution.py:15
  80.1 0.0 copy-start.3
  80.1 15.6 %fusion.9 = bf16[224,7168]{1,0:T(8,128)(2,1)} fusion(bf16[224,2048]{1,0:T(8,128)(2,1)S(1)} %all_gather.3, bf16[2048,3584]{0,1:T(8,128)(2,1)} %get-tuple-element.5, bf16[2048,3584]{0,1:T(8,128)(2,1)} %get-tuple-element.6), kind=kOutput, calls=%fused_computation.10 | convolution fusion | flops 6636994560 | bytes 33488896 | tf_op jit(solution)/shard_map/dot_general | solution.py:19
  95.7 0.0 all-reduce.2.cloned.1.call-update
  95.7 0.0 reduce-scatter.2.cloned.1.call-start
  95.8 0.0 copy-done.3
  95.8 0.1 copy.13
  95.9 124.0 %all-reduce.2.cloned.1.call-done = bf16[224,7168]{1,0:T(8,128)(2,1)} async-done(((bf16[224,7168]{1,0:T(8,128)(2,1)}), bf16[224,7168]{1,0:T(8,128)(2,1)}) %all-reduce.2.cloned.1.call-update) | async-done | bytes 3211280 | tf_op jit(solution)/shard_map/psum | solution.py:24
  219.9 2.6 convert_element_type.28
  222.5 0.1 broadcast_in_dim.22
  222.7 9.9 %broadcast_in_dim.23 = bf16[3584,16,128]{2,1,0:T(8,128)(2,1)} broadcast(bf16[3584,16]{1,0:T(8,128)(2,1)S(1)} %bitcast.27), dimensions={0,1} | broadcast | bytes 14794752 | tf_op jit(solution)/shard_map/broadcast_in_dim | solution.py:10
  232.5 14.2 %fusion.13 = bf16[224,2048]{1,0:T(8,128)(2,1)} fusion(bf16[3584,2048]{1,0:T(8,128)(2,1)} %param.10, bf16[448,8,16,128]{3,2,1,0:T(8,128)(2,1)} %bitcast.26, f32[224,7168]{1,0:T(8,128)S(1)} %convert_element_type.28), kind=kOutput, calls=%fused_computation.13 | convolution fusion | flops 3300950016 | bytes 36700160 | tf_op jit(solution)/shard_map/dot_general | solution.py:27
  246.7 0.0 reduce-scatter.2.cloned.1.call-update
  246.7 23.2 %reduce-scatter.2.cloned.1.call-done = bf16[56,2048]{1,0:T(8,128)(2,1)} async-done(((bf16[224,2048]{1,0:T(8,128)(2,1)}), bf16[56,2048]{1,0:T(8,128)(2,1)}) %reduce-scatter.2.cloned.1.call-update) | async-done | bytes 229392 | tf_op jit(solution)/shard_map/reduce_scatter | solution.py:26
  (7 shorter events, 0.1 us)
Async XLA Ops:
  6.5 213.4 %all-reduce.2.cloned.1.call-start = ((), (), s32[]{:S(2)}) async-start(), calls=%async_computation.1 | async-start | bytes 6422528 | tf_op jit(solution)/shard_map/psum | solution.py:24
  26.9 20.4 %copy-start.1 = (s32[16,28]{1,0:T(8,128)S(1)}, s32[16,28]{1,0:T(8,128)}, u32[]{:S(2)}) copy-start(s32[16,28]{1,0:T(8,128)} %param.12) | copy-start | bytes 5380
  26.9 20.7 %copy-start.2 = (s32[16,28]{1,0:T(8,128)S(1)}, s32[16,28]{1,0:T(8,128)}, u32[]{:S(2)}) copy-start(s32[16,28]{1,0:T(8,128)} %param.11) | copy-start | bytes 5380
  26.9 21.0 %copy-start = (bf16[56,2048]{1,0:T(8,128)(2,1)S(1)}, bf16[56,2048]{1,0:T(8,128)(2,1)}, u32[]{:S(2)}) copy-start(bf16[56,2048]{1,0:T(8,128)(2,1)} %param.7) | copy-start | bytes 688132
  80.1 15.7 %copy-start.3 = (s32[28,16]{0,1:T(8,128)S(1)}, s32[28,16]{0,1:T(8,128)}, u32[]{:S(2)}) copy-start(s32[28,16]{0,1:T(8,128)} %param.13) | copy-start | bytes 5380
  95.7 174.1 %reduce-scatter.2.cloned.1.call-start = ((), (), s32[]{:S(2)}) async-start(), calls=%async_computation.2 | async-start | bytes 1146880 | tf_op jit(solution)/shard_map/reduce_scatter | solution.py:26
Sparse Core Ops, SparseCore 0:
  95.9 123.9 all-reduce.1
  246.8 22.9 reduce-scatter.1
where the time goes:
time: 278 us; the launch traced here: 277 us
  waiting for transfers between devices  147 us (53%)
  local copies, waits for them, and re-layouts  51.4 us (18%)
  matrix products  29.8 us (11%)
  other arithmetic  24.1 us (9%)
  between operations  13.5 us (5%)
  blocking collectives  10.8 us (4%)
    psum x1, waiting for transfers between devices, shards(): lax.psum(partial_value.astype(jnp.bfloat16), 'feat').astype(jnp.float32)  124 us
    unnamed x16, local copies, waits for them, and re-layouts  41.1 us
    reduce_scatter x1, waiting for transfers between devices, shards(): lax.psum_scatter(jnp.dot(hidden, down_kept, preferred_element_type=jnp.fl...  23.2 us
    mul x1, other arithmetic, shards(): up_kept = up_weight * expand(up_mask)  21.4 us
    dot_general x1, matrix products, shards(): jnp.dot(lax.all_gather(tokens, ('tok', 'rep'), axis=0, tiled=True), stack...  15.6 us
    dot_general x1, matrix products, shards(): jnp.dot(hidden, down_kept, preferred_element_type=jnp.float32)  14.2 us
    all_gather x1, blocking collectives, shards(): lax.all_gather(tokens, ('tok', 'rep'), axis=0, tiled=True)  10.8 us
    broadcast_in_dim x1, local copies, waits for them, and re-layouts, expand(): jnp.repeat(jnp.repeat(mask_grid.astype(jnp.bfloat16), BLOCK, 0), BLOCK, 1)  9.86 us
  transfers between devices with their start and end apart: 2, of which 2 were waited for; matrix products, arithmetic and copies ran while one was open for 0% of the time, Pallas kernels for 0%

commit v1 on v0

v1 whole, which is shorter than its diff:
```python
import functools

import jax
import jax.numpy as jnp
from jax import lax
from jax.experimental import pallas as pl
from jax.experimental.pallas import tpu as pltpu
from jax.sharding import PartitionSpec as P

BLOCK = 128
HOP = 2
BACK = 1
EARLY = 2
MESH = pl.DeviceIdType.MESH


def kernel(nf, nx, nr, tokens, gate_w, up_w, down_w, gate_m, up_m, down_m, out,
           arrived, tok, wgu, wd, sums, part, taken, hid, acc, leaving, coming,
           tok_send, tok_recv, own_sem, g_sem, u_sem, d_sem, part_send, part_recv,
           hid_send, hid_recv, out_send, out_recv):
    z, x, r = lax.axis_index("feat"), lax.axis_index("tok"), lax.axis_index("rep")
    rows = arrived.shape[1]
    feats = tok.shape[2]
    chunks = wgu.shape[0]
    width = wd.shape[1]
    up_chunks, down_chunks = (chunks + 1) // 2, chunks // 2
    early = min(EARLY, down_chunks)
    peers = [(g, q) for g in range(nx) for q in range(nr)]

    def chip(g):
        return lax.rem(x + 1 + g, nx)

    barrier = pltpu.get_barrier_semaphore()
    for g in range(nx - 1):
        for q in range(nr):
            pl.semaphore_signal(barrier, inc=1, device_id={"tok": chip(g), "rep": q}, device_id_type=MESH)
    for step in range(1, nr):
        pl.semaphore_signal(barrier, inc=1, device_id={"rep": lax.rem(r + step, nr)}, device_id_type=MESH)

    @pl.when(z > 0)
    def _():
        pl.semaphore_signal(barrier, inc=1, device_id={"feat": z - 1}, device_id_type=MESH)

    @pl.when(z < nf - 1)
    def _():
        pl.semaphore_signal(barrier, inc=1, device_id={"feat": z + 1}, device_id_type=MESH)

    def gate_copy(j):
        cols = pl.ds(pl.multiple_of(j * width, width), width)
        return pltpu.make_async_copy(gate_w.at[:, cols], wgu.at[j, :, pl.ds(0, width)], g_sem.at[j])

    def up_copy(j):
        cols = pl.ds(pl.multiple_of(j * width, width), width)
        return pltpu.make_async_copy(up_w.at[:, cols], wgu.at[j, :, pl.ds(width, width)], u_sem.at[j])

    def down_copy(j):
        at = pl.ds(pl.multiple_of(j * width, width), width)
        return pltpu.make_async_copy(down_w.at[at, :], wd.at[j], d_sem.at[j])

    own_copy = pltpu.make_async_copy(tokens, arrived.at[(nx - 1) * nr + r], own_sem)
    own_copy.start()
    for c in range(up_chunks):
        for j in ([c, up_chunks + c] if c < down_chunks else [c]):
            gate_copy(j).start()
            up_copy(j).start()
    for c in range(up_chunks):
        for j in ([c, up_chunks + c] if c < down_chunks else [c]):
            down_copy(j).start()
    acc[...] = jnp.zeros_like(acc)

    ends = (z == 0).astype(jnp.int32) + (z == nf - 1).astype(jnp.int32)
    pl.semaphore_wait(barrier, nx * nr + 1 - ends)

    def near_copy(step):
        return pltpu.make_async_remote_copy(
            src_ref=tokens, dst_ref=arrived.at[(nx - 1) * nr + r],
            send_sem=tok_send.at[(nx - 1) * nr + step], recv_sem=tok_recv.at[(nx - 1) * nr + r],
            device_id={"rep": lax.rem(r + step, nr)}, device_id_type=MESH)

    def far_copy(g, q):
        slot = (nx - 2 - g) * nr + r
        return pltpu.make_async_remote_copy(
            src_ref=tokens, dst_ref=arrived.at[slot],
            send_sem=tok_send.at[g * nr + q], recv_sem=tok_recv.at[slot],
            device_id={"tok": chip(g), "rep": q}, device_id_type=MESH)

    def landed(slot):
        pltpu.make_async_remote_copy(
            src_ref=tokens, dst_ref=arrived.at[slot],
            send_sem=tok_send.at[0], recv_sem=tok_recv.at[slot],
            device_id={"rep": lax.rem(r + 1, nr)}, device_id_type=MESH).wait_recv()

    for step in range(1, nr):
        near_copy(step).start()
    for g in range(nx - 1):
        for q in range(nr):
            far_copy(g, q).start()
    own_copy.wait()
    for step in range(1, nr):
        landed((nx - 1) * nr + lax.rem(r + step, nr))
    for q in range(nr):
        tok[nx - 1, q * rows:(q + 1) * rows, :] = arrived[(nx - 1) * nr + q]

    def place(d):
        p = jnp.where(d == 0, z, nf - 1 - z)
        count = up_chunks if up_chunks == down_chunks else jnp.where(d == 0, up_chunks, down_chunks)
        return p, count, nx * count

    def unit(u, d, count):
        mine = (u < early) | (u >= early + (nx - 1) * count)
        other = jnp.maximum(u - early, 0)
        group = jnp.where(mine, nx - 1, other // count)
        c = jnp.where(u < early, u, jnp.where(mine, u - (nx - 1) * count, other % count))
        first = (u < early) | ((u >= 2 * early) & (u < early + count))
        return group, d * up_chunks + c, first

    def ahead(d):
        return z + 1 - 2 * d

    def behind(d):
        return z - 1 + 2 * d

    def part_copy(d, u):
        return pltpu.make_async_remote_copy(
            src_ref=part.at[d, u], dst_ref=taken.at[d, u],
            send_sem=part_send.at[d, u], recv_sem=part_recv.at[d, u],
            device_id={"feat": ahead(d)}, device_id_type=MESH)

    def hid_copy(d, u):
        return pltpu.make_async_remote_copy(
            src_ref=hid.at[d, u], dst_ref=hid.at[d, u],
            send_sem=hid_send.at[d, u], recv_sem=hid_recv.at[d, u],
            device_id={"feat": behind(d)}, device_id_type=MESH)

    def splat(scalar, shape):
        return jnp.full(shape, scalar.astype(jnp.float32)).astype(jnp.bfloat16)

    def first_half(i, d):
        p, count, units = place(d)
        u = i - HOP * p

        @pl.when((u >= 0) & (u < units))
        def _():
            group, j, first = unit(u, d, count)

            @pl.when(first)
            def _():
                gate_copy(j).wait()
                up_copy(j).wait()

            total = None
            deep = 2 * BLOCK if feats % (2 * BLOCK) == 0 else BLOCK
            for lo in range(0, feats, deep):
                tall = []
                for b in range(lo // BLOCK, (lo + deep) // BLOCK):
                    wide = []
                    for n in range(2 * width // BLOCK):
                        mask = gate_m if n < width // BLOCK else up_m
                        keep = mask[b, j * (width // BLOCK) + n % (width // BLOCK)]
                        wide.append(wgu[j, b * BLOCK:(b + 1) * BLOCK, n * BLOCK:(n + 1) * BLOCK] * splat(keep, (BLOCK, BLOCK)))
                    tall.append(jnp.concatenate(wide, axis=1))
                product = jnp.dot(tok[group, :, lo:lo + deep], jnp.concatenate(tall, axis=0),
                                  preferred_element_type=jnp.float32)
                total = product if total is None else total + product
            sums[...] = total

            @pl.when(p > 0)
            def _():
                part_copy(d, u).wait_recv()
                sums[...] += taken[d, u].astype(jnp.float32)

            @pl.when(p < nf - 1)
            def _():
                part[d, u] = sums[...].astype(jnp.bfloat16)
                part_copy(d, u).start()

            @pl.when(p == nf - 1)
            def _():
                gate, up = sums[:, :width], sums[:, width:]
                hid[d, u] = (gate / (1.0 + jnp.exp(-gate)) * up).astype(jnp.bfloat16)
                hid_copy(d, u).start()

    def second_half(i, d):
        p, count, units = place(d)
        h = i - HOP * (nf - 1) - BACK * (nf - 1 - p)

        @pl.when((h >= 0) & (h < units))
        def _():
            group, j, first = unit(h, d, count)

            @pl.when(p < nf - 1)
            def _():
                hid_copy(d, h).wait_recv()

                @pl.when(p > 0)
                def _():
                    hid_copy(d, h).start()

            @pl.when(first)
            def _():
                down_copy(j).wait()

            for n in range(wd.shape[2] // BLOCK // 2):
                cols = slice(2 * n * BLOCK, 2 * (n + 1) * BLOCK)
                tall = []
                for b in range(width // BLOCK):
                    wide = []
                    for m in (2 * n, 2 * n + 1):
                        keep = down_m[j * (width // BLOCK) + b, m]
                        wide.append(wd[j, b * BLOCK:(b + 1) * BLOCK, m * BLOCK:(m + 1) * BLOCK] * splat(keep, (BLOCK, BLOCK)))
                    tall.append(jnp.concatenate(wide, axis=1))
                acc[group, :, cols] += jnp.dot(hid[d, h], jnp.concatenate(tall, axis=0),
                                               preferred_element_type=jnp.float32)

    def out_copy(g, q):
        slot = g * nr + r
        return pltpu.make_async_remote_copy(
            src_ref=leaving.at[g * nr + q], dst_ref=coming.at[slot],
            send_sem=out_send.at[g * nr + q], recv_sem=out_recv.at[slot],
            device_id={"tok": chip(g), "rep": q}, device_id_type=MESH)

    def last_copy(step):
        return pltpu.make_async_remote_copy(
            src_ref=leaving.at[(nx - 1) * nr + step], dst_ref=coming.at[(nx - 1) * nr + r],
            send_sem=out_send.at[(nx - 1) * nr + step], recv_sem=out_recv.at[(nx - 1) * nr + r],
            device_id={"rep": lax.rem(r + step, nr)}, device_id_type=MESH)

    starts = HOP * jnp.minimum(z, nf - 1 - z) + early

    @pl.loop(0, nx * up_chunks + (HOP + BACK) * (nf - 1))
    def _(i):
        @pl.when(i == starts)
        def _():
            for g in range(nx - 1):
                for q in range(nr):
                    landed(g * nr + q)
                    tok[g, q * rows:(q + 1) * rows, :] = arrived[g * nr + q]

        @pl.loop(0, 2)
        def _(d):
            first_half(i, d)

        @pl.loop(0, 2)
        def _(d):
            second_half(i, d)

        for g in range(nx - 1):
            ends = [early + (g + 1) * count - 1 + HOP * (nf - 1) + BACK * (nf - 1 - p)
                    for count, p in ((up_chunks, z), (down_chunks, nf - 1 - z))]

            @pl.when(i == jnp.maximum(*ends))
            def _():
                for q in range(nr):
                    leaving[g * nr + q] = acc[g, q * rows:(q + 1) * rows, :].astype(jnp.bfloat16)
                    out_copy(g, q).start()

    for step in range(1, nr):
        at = pl.ds(pl.multiple_of(lax.rem(r + step, nr) * rows, 8), rows)
        leaving[(nx - 1) * nr + step] = acc[nx - 1, at, :].astype(jnp.bfloat16)
        last_copy(step).start()
    final = acc[nx - 1, pl.ds(pl.multiple_of(r * rows, 8), rows), :]

    def summed(slot):
        pltpu.make_async_remote_copy(
            src_ref=leaving.at[0], dst_ref=coming.at[slot],
            send_sem=out_send.at[0], recv_sem=out_recv.at[slot],
            device_id={"rep": lax.rem(r + 1, nr)}, device_id_type=MESH).wait_recv()
        return coming[slot].astype(jnp.float32)

    for slot in range((nx - 1) * nr):
        final += summed(slot)
    for step in range(1, nr):
        final += summed((nx - 1) * nr + lax.rem(r + step, nr))
    out[...] = final.astype(out.dtype)

    for step in range(1, nr):
        near_copy(step).wait_send()
        last_copy(step).wait_send()
    for g in range(nx - 1):
        for q in range(nr):
            far_copy(g, q).wait_send()
            out_copy(g, q).wait_send()

    @pl.loop(0, 2)
    def _(d):
        p, count, units = place(d)

        @pl.loop(0, nx * up_chunks)
        def _(u):
            @pl.when((u < units) & (p < nf - 1))
            def _():
                part_copy(d, u).wait_send()

            @pl.when((u < units) & (p > 0))
            def _():
                hid_copy(d, u).wait_send()


def solution(mesh):
    nf, nx, nr = mesh.shape["feat"], mesh.shape["tok"], mesh.shape["rep"]

    def shards(tokens, gate_weight, up_weight, down_weight, gate_mask, up_mask, down_mask):
        rows, feats = tokens.shape
        hidden = gate_weight.shape[1]
        width = 2 * BLOCK if hidden % (4 * BLOCK) == 0 else BLOCK
        chunks = hidden // width
        units = nx * ((chunks + 1) // 2)
        high = nr * rows
        bf16, f32 = jnp.bfloat16, jnp.float32
        dma = pltpu.SemaphoreType.DMA
        hbm, smem = pl.BlockSpec(memory_space=pl.ANY), pl.BlockSpec(memory_space=pltpu.SMEM)
        return pl.pallas_call(
            functools.partial(kernel, nf, nx, nr),
            out_shape=jax.ShapeDtypeStruct((rows, feats), bf16),
            in_specs=[hbm] * 4 + [smem] * 3,
            out_specs=pl.BlockSpec(memory_space=pltpu.VMEM),
            scratch_shapes=[
                pltpu.VMEM((nx * nr, rows, feats), bf16),
                pltpu.VMEM((nx, high, feats), bf16),
                pltpu.VMEM((chunks, feats, 2 * width), bf16),
                pltpu.VMEM((chunks, width, feats), bf16),
                pltpu.VMEM((high, 2 * width), f32),
                pltpu.VMEM((2, units, high, 2 * width), bf16),
                pltpu.VMEM((2, units, high, 2 * width), bf16),
                pltpu.VMEM((2, units, high, width), bf16),
                pltpu.VMEM((nx, high, feats), f32),
                pltpu.VMEM((nx * nr, rows, feats), bf16),
                pltpu.VMEM((nx * nr, rows, feats), bf16),
                dma((nx * nr,)), dma((nx * nr,)), dma(()),
                dma((chunks,)), dma((chunks,)), dma((chunks,)),
                dma((2, units)), dma((2, units)), dma((2, units)), dma((2, units)),
                dma((nx * nr,)), dma((nx * nr,)),
            ],
            compiler_params=pltpu.CompilerParams(
                collective_id=0, has_side_effects=True, vmem_limit_bytes=63 * 1024 * 1024),
        )(tokens, gate_weight, up_weight, down_weight, gate_mask, up_mask, down_mask)

    return jax.shard_map(
        shards,
        mesh=mesh,
        in_specs=(
            P(("groups", "tok", "rep"), "feat"),
            P("feat", ("tok", "rep")),
            P("feat", ("tok", "rep")),
            P(("tok", "rep"), "feat"),
            P("feat", ("tok", "rep")),
            P("feat", ("tok", "rep")),
            P(("tok", "rep"), "feat"),
        ),
        out_specs=P(("groups", "tok", "rep"), "feat"),
        check_vma=False,
    )
```

time: 278 us -> 95.4 us (0.34)
  waiting for transfers between devices: 147 us -> 0 us
  Pallas kernels: 0 us -> 92.1 us
  local copies, waits for them, and re-layouts: 51.4 us -> 3.02 us
  matrix products: 29.8 us -> 0 us
  other arithmetic: 24.1 us -> 0 us
  between operations: 13.5 us -> 0.01 us
  blocking collectives: 10.8 us -> 0 us
    psum x1 -> x0, waiting for transfers between devices: 124 us -> none  [shards(): lax.psum(partial_value.astype(jnp.bfloat16), 'feat').astype(jnp.float32)]
    pallas_call x0 -> x1, Pallas kernels: none -> 92.1 us  [shards(): pl.pallas_call(functools.partial(kernel, nf, nx, nr), out_shape=jax.Shape...]
    unnamed x16 -> x2, local copies, waits for them, and re-layouts: 41.1 us -> 3.02 us
    dot_general x2 -> x0, matrix products: 29.8 us -> none  [the longest x1 15.6 us: shards(): jnp.dot(lax.all_gather(tokens, ('tok', 'rep'), axis=0, tiled=True), stack...]
    reduce_scatter x1 -> x0, waiting for transfers between devices: 23.2 us -> none  [shards(): lax.psum_scatter(jnp.dot(hidden, down_kept, preferred_element_type=jnp.fl...]
    mul x1 -> x0, other arithmetic: 21.4 us -> none  [shards(): up_kept = up_weight * expand(up_mask)]
    all_gather x1 -> x0, blocking collectives: 10.8 us -> none  [shards(): lax.all_gather(tokens, ('tok', 'rep'), axis=0, tiled=True)]
    broadcast_in_dim x2 -> x0, local copies, waits for them, and re-layouts: 9.98 us -> none  [the longest x1 9.86 us: expand(): jnp.repeat(jnp.repeat(mask_grid.astype(jnp.bfloat16), BLOCK, 0), BLOCK, 1)]
  transfers between devices with their start and end apart: 2 -> 0, of which waited for: 2 -> 0; matrix products, arithmetic and copies ran while one was open for 0% -> 0% of each run, Pallas kernels for 0% -> 0%
where the time goes in v1:
time: 95.4 us; the launch traced here: 95.1 us
  Pallas kernels  92.1 us (97%)
  local copies, waits for them, and re-layouts  3.02 us (3%)
    pallas_call x1, Pallas kernels, shards(): pl.pallas_call(functools.partial(kernel, nf, nx, nr), out_shape=jax.Shape...  92.1 us
    unnamed x2, local copies, waits for them, and re-layouts  3.02 us

profile of v1, /device:TPU:0, one launch (start us, length us, event | category | flops | bytes accessed | tf_op | source)
XLA Modules:
  0.0 95.1 jit_solution(2240148968266911146)
XLA Ops:
  0.0 1.4 %copy.8.down_m = s32[28,16]{1,0:T(8,128)} copy(s32[28,16]{0,1:T(8,128)} %param.13) | data formatting | bytes 3584 | tf_op args[6]
  1.4 92.1 %shard_map.73 = bf16[56,2048]{1,0:T(8,128)(2,1)} custom-call(bf16[56,2048]{1,0:T(8,128)(2,1)} %tokens.1, bf16[2048,3584]{1,0:T(8,128)(2,1)} %gate_w.1, bf16[2048,3584]{1,0:T(8,128)(2,1)} %up_w.1, bf16[3584,2048]{1,0:T(8,128)(2,1)} %down_w.1, s32[16,28]{1,0:T(8,128)} %gate_m.1, s32[16,28]{1,0:T(8,128)} %up_m.1, s32[28,16]{1,0:T(8,128)} %copy.8.down_m), custom_call_target="tpu_custom_call" | custom-call | tf_op jit(solution)/shard_map/pallas_call | solution.py:312
  93.5 1.6 %copy.10 = bf16[56,2048]{1,0:T(8,128)(2,1)} copy(bf16[56,2048]{1,0:T(8,128)(2,1)} %shard_map.73) | data formatting | bytes 458752

commit v2 on v1

--- a/solution.py
+++ b/solution.py
@@ -9,7 +9,9 @@
 
 BLOCK = 128
 HOP = 2
-BACK = 1
+BACK = 2
+LEAD = 2
+DELAY = 3
 EARLY = 2
 MESH = pl.DeviceIdType.MESH
 
@@ -59,13 +61,20 @@
 
     own_copy = pltpu.make_async_copy(tokens, arrived.at[(nx - 1) * nr + r], own_sem)
     own_copy.start()
-    for c in range(up_chunks):
-        for j in ([c, up_chunks + c] if c < down_chunks else [c]):
-            gate_copy(j).start()
-            up_copy(j).start()
-    for c in range(up_chunks):
-        for j in ([c, up_chunks + c] if c < down_chunks else [c]):
-            down_copy(j).start()
+
+    def fetch(c, make):
+        make(c).start()
+        if up_chunks == down_chunks:
+            make(up_chunks + c).start()
+        else:
+            @pl.when(c < down_chunks)
+            def _():
+                make(up_chunks + c).start()
+
+    lead = min(LEAD, up_chunks)
+    for c in range(lead):
+        fetch(jnp.int32(c), gate_copy)
+        fetch(jnp.int32(c), up_copy)
     acc[...] = jnp.zeros_like(acc)
 
     ends = (z == 0).astype(jnp.int32) + (z == nf - 1).astype(jnp.int32)
@@ -178,11 +187,10 @@
             def _():
                 gate, up = sums[:, :width], sums[:, width:]
                 hid[d, u] = (gate / (1.0 + jnp.exp(-gate)) * up).astype(jnp.bfloat16)
-                hid_copy(d, u).start()
 
     def second_half(i, d):
         p, count, units = place(d)
-        h = i - HOP * (nf - 1) - BACK * (nf - 1 - p)
+        h = i - HOP * (nf - 1) - DELAY - BACK * (nf - 1 - p)
 
         @pl.when((h >= 0) & (h < units))
         def _():
@@ -192,9 +200,9 @@
             def _():
                 hid_copy(d, h).wait_recv()
 
-                @pl.when(p > 0)
-                def _():
-                    hid_copy(d, h).start()
+            @pl.when(p > 0)
+            def _():
+                hid_copy(d, h).start()
 
             @pl.when(first)
             def _():
@@ -206,7 +214,7 @@
                 for b in range(width // BLOCK):
                     wide = []
                     for m in (2 * n, 2 * n + 1):
-                        keep = down_m[j * (width // BLOCK) + b, m]
+                        keep = down_m[m, j * (width // BLOCK) + b]
                         wide.append(wd[j, b * BLOCK:(b + 1) * BLOCK, m * BLOCK:(m + 1) * BLOCK] * splat(keep, (BLOCK, BLOCK)))
                     tall.append(jnp.concatenate(wide, axis=1))
                 acc[group, :, cols] += jnp.dot(hid[d, h], jnp.concatenate(tall, axis=0),
@@ -227,7 +235,7 @@
 
     starts = HOP * jnp.minimum(z, nf - 1 - z) + early
 
-    @pl.loop(0, nx * up_chunks + (HOP + BACK) * (nf - 1))
+    @pl.loop(0, nx * up_chunks + (HOP + BACK) * (nf - 1) + DELAY)
     def _(i):
         @pl.when(i == starts)
         def _():
@@ -236,6 +244,15 @@
                     landed(g * nr + q)
                     tok[g, q * rows:(q + 1) * rows, :] = arrived[g * nr + q]
 
+        @pl.when(i + lead < up_chunks)
+        def _():
+            fetch(i + lead, gate_copy)
+            fetch(i + lead, up_copy)
+
+        @pl.when(i < up_chunks)
+        def _():
+            fetch(i, down_copy)
+
         @pl.loop(0, 2)
         def _(d):
             first_half(i, d)
@@ -245,7 +262,7 @@
             second_half(i, d)
 
         for g in range(nx - 1):
-            ends = [early + (g + 1) * count - 1 + HOP * (nf - 1) + BACK * (nf - 1 - p)
+            ends = [early + (g + 1) * count - 1 + HOP * (nf - 1) + DELAY + BACK * (nf - 1 - p)
                     for count, p in ((up_chunks, z), (down_chunks, nf - 1 - z))]
 
             @pl.when(i == jnp.maximum(*ends))
@@ -333,7 +350,7 @@
             ],
             compiler_params=pltpu.CompilerParams(
                 collective_id=0, has_side_effects=True, vmem_limit_bytes=63 * 1024 * 1024),
-        )(tokens, gate_weight, up_weight, down_weight, gate_mask, up_mask, down_mask)
+        )(tokens, gate_weight, up_weight, down_weight, gate_mask, up_mask, down_mask.T)
 
     return jax.shard_map(
         shards,

time: 95.4 us -> 82.4 us (0.86)
  Pallas kernels: 92.1 us -> 79.9 us
  local copies, waits for them, and re-layouts: 3.02 us -> 1.64 us
    pallas_call x1, Pallas kernels: 92.1 us -> 79.9 us  [shards(): pl.pallas_call(functools.partial(kernel, nf, nx, nr), out_shape=jax.Shape...]
    unnamed x2 -> x1, local copies, waits for them, and re-layouts: 3.02 us -> 1.64 us
where the time goes in v2:
time: 82.4 us; the launch traced here: 81.5 us
  Pallas kernels  79.9 us (97%)
  local copies, waits for them, and re-layouts  1.64 us (2%)
    pallas_call x1, Pallas kernels, shards(): pl.pallas_call(functools.partial(kernel, nf, nx, nr), out_shape=jax.Shape...  79.9 us

profile of v2, /device:TPU:0, one launch (start us, length us, event | category | flops | bytes accessed | tf_op | source)
XLA Modules:
  0.0 81.5 jit_solution(1278977928779554367)
XLA Ops:
  0.0 79.9 %shard_map.73 = bf16[56,2048]{1,0:T(8,128)(2,1)} custom-call(bf16[56,2048]{1,0:T(8,128)(2,1)} %tokens.1, bf16[2048,3584]{1,0:T(8,128)(2,1)} %gate_w.1, bf16[2048,3584]{1,0:T(8,128)(2,1)} %up_w.1, bf16[3584,2048]{1,0:T(8,128)(2,1)} %down_w.1, s32[16,28]{1,0:T(8,128)} %gate_m.1, s32[16,28]{1,0:T(8,128)} %up_m.1, s32[16,28]{1,0:T(8,128)} %bitcast.1), custom_call_target="tpu_custom_call" | custom-call | tf_op jit(solution)/shard_map/pallas_call | solution.py:329
  79.9 1.6 %copy.9 = bf16[56,2048]{1,0:T(8,128)(2,1)} copy(bf16[56,2048]{1,0:T(8,128)(2,1)} %shard_map.73) | data formatting | bytes 458752
